TPU v7x, 32 devices: a whole 2x2x4 slice. The times are simulated.
32 devices in a mesh: groups: 2 (over x), label: 8 (over z, y), cent: 2 (over core).
Axes of the slice: x: 2, y: 2, z: 4, core: 2. Of those that a mesh axis runs over, the one named last changes fastest.
Arguments:
- embeddings: bfloat16 [768, 16384], P('label', 'groups'), parts along dimension 1, may hold values from -40 to 40
- centroids: bfloat16 [2, 8192, 768], P('cent', ('groups', 'label')), parts along dimension 1, may hold values from -1 to 1
Outputs:
- new_centroids: float32 [2, 8192, 768], P('cent', ('groups', 'label')), parts along dimension 1
There are 2 independent parts, one for each index of `groups`. A program takes and returns all parts, laid end to end along the dimension named above; each array names one. Nothing has to cross between parts.
All inputs are finite; a program needn't handle non-finite values.
Results may differ from a plain program's by a relative error of at most 0.012.
Values may be sent and summed in bfloat16 or wider, within the bound.
A program may use at most 128 MiB of HBM per device.

v0:
```python
import jax
import jax.numpy as jnp
from jax import lax
from jax.sharding import PartitionSpec as P

prior_weight = 1.0


def weights_cent(scores):
    row_top = lax.pmax(jnp.max(scores, axis=1), "cent")
    exponent = jnp.exp(scores - row_top[:, None])
    row_sum = lax.psum(jnp.sum(exponent, axis=1), "cent")
    return (exponent / row_sum[:, None]).astype(jnp.bfloat16)


def score_against(feature_table, centroid_slice):
    half_norms = 0.5 * jnp.sum(jnp.square(centroid_slice.astype(jnp.float32)), axis=1)
    products = lax.dot_general(
        feature_table, centroid_slice, (((0,), (1,)), ((), ())), preferred_element_type=jnp.float32
    )
    return products - half_norms[None, :]


def weighted_sums(weights, feature_table):
    partial_terms = lax.dot_general(
        weights, feature_table, (((0,), (1,)), ((), ())), preferred_element_type=jnp.float32
    )
    counts = jnp.sum(weights, axis=0, dtype=jnp.float32)
    return (partial_terms, counts)


def body(embeddings, centroids):
    held_centroids = centroids[0]
    relaid = lax.all_to_all(embeddings, "label", split_axis=1, concat_axis=0, tiled=True)
    scores = score_against(relaid, lax.all_gather(centroids, "label", axis=1, tiled=True)[0])
    weights = weights_cent(scores)
    partial_terms, counts = weighted_sums(weights, relaid)
    numerators, totals = (
        lax.psum_scatter(
            partial_terms.astype(jnp.bfloat16), "label", scatter_dimension=0, tiled=True
        ).astype(jnp.float32),
        lax.psum_scatter(
            counts.astype(jnp.bfloat16), "label", scatter_dimension=0, tiled=True
        ).astype(jnp.float32),
    )
    updated = (numerators + prior_weight * held_centroids.astype(jnp.float32)) / (
        totals + prior_weight
    )[:, None]
    return updated[None]


def solution(mesh):
    return jax.shard_map(
        body,
        mesh=mesh,
        in_specs=(P("label", "groups"), P("cent", ("groups", "label"), None)),
        out_specs=P("cent", ("groups", "label"), None),
        check_vma=False,
    )
```

profile of v0, /device:TPU:0, one launch (start us, length us, event | category | flops | bytes accessed | tf_op | source)
XLA Modules:
  0.0 312.0 jit_solution(1574253930327543209)
XLA Ops:
  6.5 0.0 all-gather.2.cloned.1.call-start
  6.5 0.7 all-gather.2.cloned.1.call-update
  7.3 2.7 copy.7
  10.0 7.3 %all-to-all-start = ((bf16[96,8,1024]{2,0,1:T(8,128)(2,1)}), bf16[96,8,1024]{2,0,1:T(8,128)(2,1)S(1)}, u32[]{:S(2)}, u32[]{:S(2)}) async-start(bf16[96,8,1024]{2,0,1:T(8,128)(2,1)} %bitcast.21), calls=%async_computation | async-start | bytes 3145728 | tf_op jit(solution)/shard_map/all_to_all | solution.py:34
  17.3 0.0 reduce-scatter.2.cloned.1.call-start
  17.3 121.1 %all-gather.2.cloned.1.call-done = bf16[1,4096,768]{2,1,0:T(8,128)(2,1)} async-done(((bf16[1,512,768]{2,1,0:T(8,128)(2,1)}), bf16[1,4096,768]{2,1,0:T(8,128)(2,1)}) %all-gather.2.cloned.1.call-update) | async-done | bytes 6291472 | tf_op jit(solution)/shard_map/all_gather | solution.py:35
  138.4 4.1 %multiply_reduce_fusion = f32[4096]{0:T(1024)S(1)} fusion(bf16[1,4096,768]{2,1,0:T(8,128)(2,1)} %all-gather.2.cloned.1.call-done), kind=kLoop, calls=%fused_computation.4 | loop fusion | flops 9433088 | bytes 6307840 | tf_op jit(solution)/shard_map/reduce_sum | solution.py:17
  142.5 0.0 all-to-all-done
  142.6 13.1 %subtract_reduce_fusion = (f32[1024]{0:T(1024)S(1)}, f32[1024,4096]{1,0:T(8,128)}) fusion(f32[4096]{0:T(1024)S(1)} %broadcast_multiply_fusion, bf16[768,1024]{1,0:T(8,128)(2,1)S(1)} %bitcast.23, bf16[1,4096,768]{2,1,0:T(8,128)(2,1)} %all-gather.2.cloned.1.call-done), kind=kOutput, calls=%fused_computation.2 | convolution fusion | flops 6450838528 | bytes 24662016 | tf_op jit(solution)/shard_map/dot_general | solution.py:18
  155.6 2.4 pmax.7
  158.1 8.6 %fusion = f32[1024]{0:T(1024)S(1)} fusion(f32[1024,4096]{1,0:T(8,128)} %get-tuple-element.8, f32[1024]{0:T(1024)S(1)} %pmax.7, f32[4096]{0:T(1024)S(1)} %broadcast_multiply_fusion), kind=kLoop, calls=%fused_computation.3 | loop fusion | flops 12581888 | bytes 16801792 | tf_op jit(solution)/shard_map/reduce_sum | solution.py:12
  166.7 2.5 psum.7
  169.2 8.1 %fusion.5 = (bf16[4096]{0:T(1024)(128)(2,1)S(1)}, bf16[1024,4096]{1,0:T(8,128)(2,1)S(1)}) fusion(f32[1024]{0:T(1024)S(1)} %psum.7, f32[1024]{0:T(1024)S(1)} %pmax.7, f32[1024,4096]{1,0:T(8,128)} %get-tuple-element.8, f32[4096]{0:T(1024)S(1)} %broadcast_multiply_fusion), kind=kLoop, calls=%fused_computation.14 | loop fusion | flops 20967424 | bytes 25198592 | tf_op jit(solution)/shard_map/reduce_sum | solution.py:28
  177.2 0.0 copy-start.1
  177.3 0.0 copy-start
  177.3 9.0 %convolution_convert_fusion = bf16[4096,768]{1,0:T(8,128)(2,1)} fusion(bf16[1024,4096]{1,0:T(8,128)(2,1)S(1)} %get-tuple-element.6, bf16[768,1024]{1,0:T(8,128)(2,1)S(1)} %bitcast.24), kind=kOutput, calls=%fused_computation.5 | convolution fusion | flops 6445596672 | bytes 16252928 | tf_op jit(solution)/shard_map/dot_general | solution.py:25
  186.2 0.0 reduce-scatter.2.cloned.1.call-update
  186.3 0.0 copy-done.1
  186.3 0.6 dynamic-slice
  187.5 19.7 %all-reduce = bf16[4096]{0:T(1024)(128)(2,1)S(1)} all-reduce(bf16[4096]{0:T(1024)(128)(2,1)S(1)} %get-tuple-element.5), channel_id=3, replica_groups=mesh['groups'=2,'label'=8,'cent'=2] {'label'}, use_global_device_ids=true, to_apply=%region_7.0.clone | all-reduce | flops 4096 | bytes 16384
  207.3 0.1 convert_add_fusion.1
  207.3 95.3 %reduce-scatter.2.cloned.1.call-done = bf16[512,768]{1,0:T(8,128)(2,1)} async-done(((bf16[4096,768]{1,0:T(8,128)(2,1)}), bf16[512,768]{1,0:T(8,128)(2,1)}) %reduce-scatter.2.cloned.1.call-update) | async-done | bytes 786448 | tf_op jit(solution)/shard_map/reduce_scatter | solution.py:39
  302.6 0.0 copy-done
  302.6 2.5 fusion.4
  (1 shorter events, 0.0 us)
Async XLA Ops:
  6.5 131.9 %all-gather.2.cloned.1.call-start = ((), (), s32[]{:S(2)}) async-start(), calls=%async_computation.2 | async-start | bytes 7077888 | tf_op jit(solution)/shard_map/all_gather | solution.py:35
  10.0 132.6 %all-to-all-start = ((bf16[96,8,1024]{2,0,1:T(8,128)(2,1)}), bf16[96,8,1024]{2,0,1:T(8,128)(2,1)S(1)}, u32[]{:S(2)}, u32[]{:S(2)}) async-start(bf16[96,8,1024]{2,0,1:T(8,128)(2,1)} %bitcast.21), calls=%async_computation | async-start | bytes 3145728 | tf_op jit(solution)/shard_map/all_to_all | solution.py:34
  17.3 285.4 %reduce-scatter.2.cloned.1.call-start = ((), (), s32[]{:S(2)}) async-start(), calls=%async_computation.3 | async-start | bytes 7077888 | tf_op jit(solution)/shard_map/reduce_scatter | solution.py:39
  177.2 9.0 %copy-start.1 = (u32[32]{0:T(128)S(1)}, u32[32]{0:T(128)}, u32[]{:S(2)}) copy-start(u32[32]{0:T(128)} %constant.13) | copy-start | bytes 388
  177.3 125.4 %copy-start = (bf16[1,512,768]{2,1,0:T(8,128)(2,1)S(1)}, bf16[1,512,768]{2,1,0:T(8,128)(2,1)}, u32[]{:S(2)}) copy-start(bf16[1,512,768]{2,1,0:T(8,128)(2,1)} %param.3) | copy-start | bytes 2359300
Sparse Core Ops, SparseCore 0:
  9.5 128.8 all-gather.1
  186.4 116.2 reduce-scatter.1
where the time goes:
time: 312 us
  waiting for transfers between devices  217 us (70%)
  blocking collectives  24.6 us (8%)
  other arithmetic  23.4 us (8%)
  matrix products  22 us (7%)
  between operations  14.1 us (5%)
  starting transfers between devices  7.32 us (2%)
  local copies, waits for them, and re-layouts  3.31 us (1%)
    all_gather x1, waiting for transfers between devices, body(): lax.all_gather(centroids, 'label', axis=1, tiled=True)[0]  121 us
    reduce_scatter x1, waiting for transfers between devices, body(): lax.psum_scatter(partial_terms.astype(jnp.bfloat16), 'label', scatter_dim...  95.3 us
    unnamed x1, blocking collectives  19.7 us
    dot_general x1, matrix products, score_against(): lax.dot_general(feature_table, centroid_slice, (((0,), (1,)), ((), ())),...  13.1 us
    dot_general x1, matrix products, weighted_sums(): lax.dot_general(weights, feature_table, (((0,), (1,)), ((), ())), preferr...  8.97 us
    reduce_sum x1, other arithmetic, weights_cent(): row_sum = lax.psum(jnp.sum(exponent, axis=1), 'cent')  8.64 us
    reduce_sum x1, other arithmetic, weighted_sums(): counts = jnp.sum(weights, axis=0, dtype=jnp.float32)  8.07 us
    all_to_all x1, starting transfers between devices, body(): lax.all_to_all(embeddings, 'label', split_axis=1, concat_axis=0, tiled=True)  7.28 us
  transfers between devices with their start and end apart: 3, of which 2 were waited for; matrix products, arithmetic and copies ran while one was open for 2% of the time, Pallas kernels for 0%

commit v1 on v0

v1 whole, which is shorter than its diff:
```python
import jax
import jax.numpy as jnp
from jax import lax
from jax.sharding import PartitionSpec as P

prior_weight = 1.0


def body(embeddings, centroids):
    held = centroids[0]
    half = embeddings.shape[1] // lax.axis_size("cent")
    mine = lax.dynamic_slice_in_dim(embeddings, lax.axis_index("cent") * half, half, axis=1)
    column = lax.all_gather(mine, "label", axis=0, tiled=True)
    table = lax.all_gather(column, "cent", axis=1, tiled=True)
    half_norms = 0.5 * jnp.sum(jnp.square(held.astype(jnp.float32)), axis=1)
    scores = jnp.dot(held, table, preferred_element_type=jnp.float32) - half_norms[:, None]
    top = jnp.max(scores, axis=0)
    total = jnp.sum(jnp.exp(scores - top[None, :]), axis=0)
    tops = lax.all_gather(jnp.stack([top, total]), ("label", "cent"))
    row_top = jnp.max(tops[:, 0], axis=0)
    row_sum = jnp.sum(tops[:, 1] * jnp.exp(tops[:, 0] - row_top[None]), axis=0)
    weights = (jnp.exp(scores - row_top[None, :]) / row_sum[None, :]).astype(jnp.bfloat16)
    sums = lax.dot_general(weights, table, (((1,), (1,)), ((), ())), preferred_element_type=jnp.float32)
    counts = jnp.sum(weights, axis=1, dtype=jnp.float32)
    updated = (sums + prior_weight * held.astype(jnp.float32)) / (counts + prior_weight)[:, None]
    return updated[None]


def solution(mesh):
    return jax.shard_map(
        body,
        mesh=mesh,
        in_specs=(P("label", "groups"), P("cent", ("groups", "label"), None)),
        out_specs=P("cent", ("groups", "label"), None),
        check_vma=False,
    )
```

time: 312 us -> 235 us (0.75)
  waiting for transfers between devices: 217 us -> 165 us
  blocking collectives: 24.6 us -> 0 us
  starting transfers between devices: 7.32 us -> 0.08 us
  matrix products: 22 us -> 28.7 us
    reduce_scatter x1 -> x0, waiting for transfers between devices: 95.3 us -> none  [body(): lax.psum_scatter(partial_terms.astype(jnp.bfloat16), 'label', scatter_dim...]
    all_gather x1 -> x3, waiting for transfers between devices: 121 us -> 165 us  [the longest x1 102 us: body(): column = lax.all_gather(mine, 'label', axis=0, tiled=True)]
    unnamed x1 -> x0, blocking collectives: 19.7 us -> none
    all_to_all x1 -> x0, starting transfers between devices: 7.28 us -> none  [body(): lax.all_to_all(embeddings, 'label', split_axis=1, concat_axis=0, tiled=True)]
    dot_general x2, matrix products: 22 us -> 28.7 us  [the longest x1 14.9 us: body(): jnp.dot(held, table, preferred_element_type=jnp.float32)]
    reduce_sum x3 -> x4, other arithmetic: 20.8 us -> 22.3 us  [the longest x1 11.3 us: body(): counts = jnp.sum(weights, axis=1, dtype=jnp.float32)]
  transfers between devices with their start and end apart: 3 -> 3, of which waited for: 2 -> 3; matrix products, arithmetic and copies ran while one was open for 2% -> 1% of each run, Pallas kernels for 0% -> 0%
where the time goes in v1:
time: 235 us
  waiting for transfers between devices  165 us (70%)
  matrix products  28.7 us (12%)
  other arithmetic  25.9 us (11%)
  between operations  13.1 us (6%)
  local copies, waits for them, and re-layouts  2.35 us (1%)
    all_gather x1, waiting for transfers between devices, body(): column = lax.all_gather(mine, 'label', axis=0, tiled=True)  102 us
    all_gather x1, waiting for transfers between devices, body(): tops = lax.all_gather(jnp.stack([top, total]), ('label', 'cent'))  39.3 us
    all_gather x1, waiting for transfers between devices, body(): table = lax.all_gather(column, 'cent', axis=1, tiled=True)  23.2 us
    dot_general x1, matrix products, body(): jnp.dot(held, table, preferred_element_type=jnp.float32)  14.9 us
    dot_general x1, matrix products, body(): lax.dot_general(weights, table, (((1,), (1,)), ((), ())), preferred_eleme...  13.8 us
    reduce_sum x1, other arithmetic, body(): counts = jnp.sum(weights, axis=1, dtype=jnp.float32)  11.3 us
    reduce_sum x1, other arithmetic, body(): total = jnp.sum(jnp.exp(scores - top[None, :]), axis=0)  9.02 us
  transfers between devices with their start and end apart: 3, of which 3 were waited for; matrix products, arithmetic and copies ran while one was open for 1% of the time, Pallas kernels for 0%

profile of v1, /device:TPU:0, one launch (start us, length us, event | category | flops | bytes accessed | tf_op | source)
XLA Modules:
  0.0 235.1 jit_solution(4683139684345847898)
XLA Ops:
  6.5 0.0 copy-start
  6.5 0.0 all-gather.6.cloned.1.call-start
  6.5 1.4 copy-done
  7.9 0.9 constant_dynamic-slice_fusion
  8.9 0.0 all-gather.6.cloned.1.call-update
  8.9 0.0 all-gather.8.cloned.1.call-start
  9.0 102.4 %all-gather.6.cloned.1.call-done = bf16[768,4096]{1,0:T(8,128)(2,1)} async-done(((bf16[96,4096]{1,0:T(8,128)(2,1)}), bf16[768,4096]{1,0:T(8,128)(2,1)}) %all-gather.6.cloned.1.call-update) | async-done | bytes 6291472 | tf_op jit(solution)/shard_map/all_gather | solution.py:13
  111.3 0.0 all-gather.8.cloned.1.call-update
  111.3 0.0 all-gather.10.cloned.1.call-start
  111.4 1.4 fusion
  112.7 23.2 %all-gather.8.cloned.1.call-done = bf16[768,8192]{1,0:T(8,128)(2,1)} async-done(((bf16[768,4096]{1,0:T(8,128)(2,1)}), bf16[768,8192]{1,0:T(8,128)(2,1)}) %all-gather.8.cloned.1.call-update) | async-done | bytes 12582928 | tf_op jit(solution)/shard_map/all_gather | solution.py:14
  136.0 14.9 %subtract_reduce_fusion = (f32[8192]{0:T(1024)S(1)}, f32[8192,512]{0,1:T(8,128)}) fusion(f32[512]{0:T(512)S(1)} %broadcast_multiply_fusion, bf16[768,8192]{1,0:T(8,128)(2,1)} %all-gather.8.cloned.1.call-done, bf16[1,512,768]{2,1,0:T(8,128)(2,1)} %param.3), kind=kOutput, calls=%fused_computation.3 | convolution fusion | flops 6450831360 | bytes 30181376 | tf_op jit(solution)/shard_map/dot_general | solution.py:16
  150.9 9.0 %exponential_reduce_fusion = f32[8192]{0:T(1024)S(1)} fusion(f32[8192,512]{0,1:T(8,128)} %get-tuple-element.11, f32[8192]{0:T(1024)S(1)} %get-tuple-element.10, f32[512]{0:T(512)S(1)} %broadcast_multiply_fusion), kind=kLoop, calls=%fused_computation.2 | loop fusion | flops 12574720 | bytes 16844800 | tf_op jit(solution)/shard_map/reduce_sum | solution.py:18
  159.9 0.7 maximum_bitcast_fusion
  160.6 0.0 all-gather.10.cloned.1.call-update
  160.6 39.3 %all-gather.10.cloned.1.call-done = f32[16,2,8192]{2,1,0:T(2,128)} async-done(((f32[1,2,8192]{2,1,0:T(2,128)}), f32[16,2,8192]{2,1,0:T(2,128)}) %all-gather.10.cloned.1.call-update) | async-done | bytes 1048592 | tf_op jit(solution)/shard_map/all_gather | solution.py:19
  199.9 2.9 %slice_reduce_fusion = (f32[8192]{0:T(1024)S(1)}, f32[16,1,8192]{2,1,0:T(1,128)S(1)}, f32[16,1,8192]{2,1,0:T(1,128)S(1)}) fusion(f32[16,2,8192]{2,1,0:T(2,128)} %all-gather.10.cloned.1.call-done), kind=kLoop, calls=%fused_computation.20 | loop fusion | flops 122880 | bytes 2129920 | tf_op jit(solution)/shard_map/reduce_max | solution.py:20
  202.8 0.7 fusion.6
  203.5 0.0 copy-start.1
  203.5 11.3 %convert_reduce_fusion = (f32[512]{0:T(512)S(1)}, bf16[8192,512]{0,1:T(8,128)(2,1)}) fusion(f32[8192]{0:T(1024)S(1)} %fusion.6, f32[8192]{0:T(1024)S(1)} %get-tuple-element.7, f32[8192,512]{0,1:T(8,128)} %get-tuple-element.11, f32[512]{0:T(512)S(1)} %broadcast_multiply_fusion), kind=kLoop, calls=%fused_computation | loop fusion | flops 25165312 | bytes 25235456 | tf_op jit(solution)/shard_map/reduce_sum | solution.py:24
  214.8 0.0 copy-done.1
  214.8 13.8 %fusion.2 = f32[1,512,768]{2,1,0:T(8,128)} fusion(bf16[8192,512]{0,1:T(8,128)(2,1)} %get-tuple-element.6, bf16[768,8192]{1,0:T(8,128)(2,1)} %all-gather.8.cloned.1.call-done, bf16[1,512,768]{2,1,0:T(8,128)(2,1)S(1)} %copy-done.1, f32[512]{0:T(512)S(1)} %broadcast_add_fusion), kind=kOutput, calls=%fused_computation.8 | convolution fusion | flops 6443630592 | bytes 23332864 | tf_op jit(solution)/shard_map/dot_general | solution.py:23
  (2 shorter events, 0.0 us)
Async XLA Ops:
  6.5 1.4 copy-start
  6.5 104.8 %all-gather.6.cloned.1.call-start = ((), (), s32[]{:S(2)}) async-start(), calls=%async_computation | async-start | bytes 7077888 | tf_op jit(solution)/shard_map/all_gather | solution.py:13
  8.9 127.1 %all-gather.8.cloned.1.call-start = ((), (), s32[]{:S(2)}) async-start(), calls=%async_computation.1 | async-start | bytes 18874368 | tf_op jit(solution)/shard_map/all_gather | solution.py:14
  111.3 88.6 %all-gather.10.cloned.1.call-start = ((), (), s32[]{:S(2)}) async-start(), calls=%async_computation.2 | async-start | bytes 1114112 | tf_op jit(solution)/shard_map/all_gather | solution.py:19
  203.5 11.3 %copy-start.1 = (bf16[1,512,768]{2,1,0:T(8,128)(2,1)S(1)}, bf16[1,512,768]{2,1,0:T(8,128)(2,1)}, u32[]{:S(2)}) copy-start(bf16[1,512,768]{2,1,0:T(8,128)(2,1)} %param.3) | copy-start | bytes 2359300
Sparse Core Ops, SparseCore 0:
  9.5 101.7 all-gather.5
  112.9 23.0 all-gather.7
  160.7 39.0 all-gather.9

commit v2 on v1

--- a/solution.py
+++ b/solution.py
@@ -1,12 +1,18 @@
+import functools
 import jax
 import jax.numpy as jnp
 from jax import lax
+from jax.experimental import pallas as pl
+from jax.experimental.pallas import tpu as pltpu
 from jax.sharding import PartitionSpec as P
 
 prior_weight = 1.0
-
-
-def body(embeddings, centroids):
+COLS = 2
+CHUNK = 512
+MESH = pl.DeviceIdType.MESH
+
+
+def plain_body(embeddings, centroids):
     held = centroids[0]
     half = embeddings.shape[1] // lax.axis_size("cent")
     mine = lax.dynamic_slice_in_dim(embeddings, lax.axis_index("cent") * half, half, axis=1)
@@ -26,7 +32,227 @@
     return updated[None]
 
 
+def kernel(n_label, e_ref, c_ref, out_ref, table, expo, stats, sums, counts, norms,
+           load_sem, send_sem, recv_sem, sib_sem, stat_send, stat_recv):
+    chunks, _, width = table.shape
+    rows = e_ref.shape[0]
+    half = width // 2
+    n_z = n_label // COLS
+    n_dev = 2 * n_label
+    me = lax.axis_index("label")
+    core = lax.axis_index("cent")
+    z, y = me // COLS, me % COLS
+    self_id = me * 2 + core
+
+    def block(index):
+        return pl.ds(pl.multiple_of(index * rows, rows), rows)
+
+    loads = [
+        pltpu.make_async_copy(e_ref.at[:, pl.ds(j * width, width)], table.at[j, block(me), :], load_sem)
+        for j in range(chunks)
+    ]
+    for copy in loads:
+        copy.start()
+
+    barrier = pltpu.get_barrier_semaphore()
+
+    def greet(k, carry):
+        other = lax.rem(self_id + k, n_dev)
+        pl.semaphore_signal(barrier, inc=1, device_id={"label": other // 2, "cent": other % 2}, device_id_type=MESH)
+        return carry
+
+    lax.fori_loop(1, n_dev, greet, 0)
+
+    centroids = c_ref[...].astype(jnp.float32)
+    norms[...] = jnp.broadcast_to(0.5 * jnp.sum(centroids * centroids, axis=1, keepdims=True), norms.shape)
+    sums[...] = jnp.zeros_like(sums)
+    counts[...] = jnp.zeros_like(counts)
+    pltpu.make_async_copy(table.at[:, pl.ds(0, rows), :], table.at[:, pl.ds(0, rows), :], load_sem).wait()
+    pl.semaphore_wait(barrier, n_dev - 1)
+
+    def piece(j, index):
+        return table.at[j, block(index), pl.ds(pl.multiple_of(core * half, half), half)]
+
+    def hop(j, index, kind, target):
+        return pltpu.make_async_remote_copy(
+            src_ref=piece(j, index), dst_ref=piece(j, index), send_sem=send_sem.at[kind],
+            recv_sem=recv_sem.at[j, index], device_id={"label": target}, device_id_type=MESH)
+
+    def sibling(j, index):
+        return pltpu.make_async_remote_copy(
+            src_ref=piece(j, index), dst_ref=piece(j, index), send_sem=send_sem.at[3],
+            recv_sem=sib_sem.at[j], device_id={"cent": 1 - core}, device_id_type=MESH)
+
+    def up(j, index):
+        @pl.when(z < n_z - 1)
+        def _():
+            hop(j, index, 0, me + COLS).start()
+
+    def down(j, index):
+        @pl.when(z > 0)
+        def _():
+            hop(j, index, 1, me - COLS).start()
+
+    across_label = z * COLS + 1 - y
+
+    def across(j, index):
+        hop(j, index, 2, across_label).start()
+
+    def live(j):
+        return jnp.logical_and(j >= 0, j < chunks)
+
+    def relay(t):
+        @pl.when(t < chunks)
+        def _():
+            up(t, me)
+            down(t, me)
+            across(t, me)
+
+        for d in range(1, n_z):
+            j = t - d
+            for sign in (-1, 1):
+                far = z + sign * d
+                edge = jnp.logical_or(far == 0, far == n_z - 1)
+
+                @pl.when(live(j) & (far >= 0) & (far < n_z))
+                def _():
+                    index = far * COLS + y
+                    hop(j, index, 0, me).wait_recv()
+                    (up if sign < 0 else down)(j, index)
+
+                    @pl.when(jnp.logical_not(edge & (j % 2 == 0)))
+                    def _():
+                        across(j, index)
+
+                    sibling(j, index).start()
+
+        for d in range(n_z):
+            j = t - d - 1
+            for sign in ((1,) if d == 0 else (-1, 1)):
+                far = z + sign * d
+
+                @pl.when(live(j) & (far >= 0) & (far < n_z))
+                def _():
+                    index = far * COLS + 1 - y
+                    hop(j, index, 0, me).wait_recv()
+
+                    @pl.when((j % 2 == 0) & (far == 0))
+                    def _():
+                        up(j, index)
+
+                    @pl.when((j % 2 == 0) & (far == n_z - 1))
+                    def _():
+                        down(j, index)
+
+                    sibling(j, index).start()
+
+    def score(j):
+        others = table.at[j, pl.ds(0, (n_label - 1) * rows), pl.ds(0, half)]
+        pltpu.make_async_copy(others, others, sib_sem.at[j]).wait()
+        products = jnp.dot(c_ref[...], table[j], preferred_element_type=jnp.float32)
+        scores = products - norms[:, 0:1]
+        top = jnp.max(scores, axis=0, keepdims=True)
+        exponent = jnp.exp(scores - top)
+        expo[j] = exponent
+        stats[j, self_id, 0:1, :] = top
+        stats[j, self_id, 1:2, :] = jnp.sum(exponent, axis=0, keepdims=True)
+
+        def tell(k, carry):
+            other = lax.rem(self_id + k, n_dev)
+            pltpu.make_async_remote_copy(
+                src_ref=stats.at[j, self_id], dst_ref=stats.at[j, self_id], send_sem=stat_send,
+                recv_sem=stat_recv.at[j], device_id={"label": other // 2, "cent": other % 2},
+                device_id_type=MESH).start()
+            return carry
+
+        lax.fori_loop(1, n_dev, tell, 0)
+
+    def absorb(j):
+        others = stats.at[j, pl.ds(0, n_dev - 1)]
+        pltpu.make_async_copy(others, others, stat_recv.at[j]).wait()
+        tops = stats[j, :, 0, :]
+        row_top = jnp.max(tops, axis=0, keepdims=True)
+        row_sum = jnp.sum(stats[j, :, 1, :] * jnp.exp(tops - row_top), axis=0, keepdims=True)
+        factor = jnp.exp(stats[j, self_id, 0:1, :] - row_top) / row_sum
+        weights = (expo[j] * factor).astype(jnp.bfloat16)
+        sums[...] += lax.dot_general(
+            weights, table[j], (((1,), (1,)), ((), ())), preferred_element_type=jnp.float32)
+        part = counts[...]
+        for k in range(width // 128):
+            part += weights[:, k * 128:(k + 1) * 128].astype(jnp.float32)
+        counts[...] = part
+
+    lag_a = n_z + 1
+    lag_b = n_z + 2
+
+    def tick(t, carry):
+        relay(t)
+
+        @pl.when(live(t - lag_a))
+        def _():
+            score(t - lag_a)
+
+        @pl.when(live(t - lag_b))
+        def _():
+            absorb(t - lag_b)
+
+        return carry
+
+    lax.fori_loop(0, chunks + lag_b, tick, 0)
+
+    total = jnp.sum(counts[...], axis=1, keepdims=True)
+    out_ref[...] = (sums[...] + prior_weight * c_ref[...].astype(jnp.float32)) / (total + prior_weight)
+
+    def drain(kind, halves):
+        ref = table.at[:, pl.ds(0, halves * rows // 2), pl.ds(0, half)]
+        pltpu.make_async_copy(ref, ref, send_sem.at[kind]).wait()
+
+    for k in range(n_z):
+        @pl.when(z == k)
+        def _():
+            if k < n_z - 1:
+                drain(0, 2 * (k + 1) + 1)
+            if k > 0:
+                drain(1, 2 * (n_z - k) + 1)
+            drain(2, 2 * n_z - (1 if k in (0, n_z - 1) else 2))
+    drain(3, 2 * (n_label - 1))
+    told = stats.at[:, pl.ds(0, n_dev - 1)]
+    pltpu.make_async_copy(told, told, stat_send).wait()
+
+
+def fused_body(n_label, embeddings, centroids):
+    held = centroids[0]
+    rows, labels = embeddings.shape
+    count, depth = held.shape
+    chunks = labels // CHUNK
+    updated = pl.pallas_call(
+        functools.partial(kernel, n_label),
+        out_shape=jax.ShapeDtypeStruct((count, depth), jnp.float32),
+        in_specs=[pl.BlockSpec(memory_space=pl.ANY), pl.BlockSpec(memory_space=pltpu.VMEM)],
+        out_specs=pl.BlockSpec(memory_space=pltpu.VMEM),
+        scratch_shapes=[
+            pltpu.VMEM((chunks, depth, CHUNK), jnp.bfloat16),
+            pltpu.VMEM((chunks, count, CHUNK), jnp.float32),
+            pltpu.VMEM((chunks, 2 * n_label, 2, CHUNK), jnp.float32),
+            pltpu.VMEM((count, depth), jnp.float32),
+            pltpu.VMEM((count, 128), jnp.float32),
+            pltpu.VMEM((count, 128), jnp.float32),
+            pltpu.SemaphoreType.DMA,
+            pltpu.SemaphoreType.DMA((4,)),
+            pltpu.SemaphoreType.DMA((chunks, n_label)),
+            pltpu.SemaphoreType.DMA((chunks,)),
+            pltpu.SemaphoreType.DMA,
+            pltpu.SemaphoreType.DMA((chunks,)),
+        ],
+        compiler_params=pltpu.CompilerParams(
+            collective_id=0, has_side_effects=True, vmem_limit_bytes=60 * 1024 * 1024),
+    )(embeddings, held)
+    return updated[None]
+
+
 def solution(mesh):
+    fused = mesh.shape["label"] == 8 and mesh.shape["groups"] == 2
+    body = functools.partial(fused_body, mesh.shape["label"]) if fused else plain_body
     return jax.shard_map(
         body,
         mesh=mesh,

time: 235 us -> 99.1 us (0.42)
  waiting for transfers between devices: 165 us -> 0 us
  Pallas kernels: 0 us -> 96.2 us
  matrix products: 28.7 us -> 0 us
  other arithmetic: 25.9 us -> 0 us
  between operations: 13.1 us -> 0.01 us
    all_gather x3 -> x0, waiting for transfers between devices: 165 us -> none  [the longest x1 102 us: body(): column = lax.all_gather(mine, 'label', axis=0, tiled=True)]
    pallas_call x0 -> x1, Pallas kernels: none -> 96.2 us  [fused_body(): pl.pallas_call(functools.partial(kernel, n_label), out_shape=jax.ShapeDty...]
    dot_general x2 -> x0, matrix products: 28.7 us -> none  [the longest x1 14.9 us: body(): jnp.dot(held, table, preferred_element_type=jnp.float32)]
    reduce_sum x4 -> x0, other arithmetic: 22.3 us -> none  [the longest x1 11.3 us: body(): counts = jnp.sum(weights, axis=1, dtype=jnp.float32)]
    reduce_max x1 -> x0, other arithmetic: 2.89 us -> none  [body(): row_top = jnp.max(tops[:, 0], axis=0)]
  transfers between devices with their start and end apart: 3 -> 0, of which waited for: 3 -> 0; matrix products, arithmetic and copies ran while one was open for 1% -> 0% of each run, Pallas kernels for 0% -> 0%
where the time goes in v2:
time: 99.1 us; the launch traced here: 98.9 us
  Pallas kernels  96.2 us (97%)
  local copies, waits for them, and re-layouts  2.65 us (3%)
    pallas_call x1, Pallas kernels, fused_body(): pl.pallas_call(functools.partial(kernel, n_label), out_shape=jax.ShapeDty...  96.2 us
    unnamed x1, local copies, waits for them, and re-layouts  2.65 us

profile of v2, /device:TPU:0, one launch (start us, length us, event | category | flops | bytes accessed | tf_op | source)
XLA Modules:
  0.0 98.9 jit_solution(9896170424029596531)
XLA Ops:
  0.0 96.2 %shard_map.28 = f32[512,768]{1,0:T(8,128)} custom-call(bf16[96,8192]{1,0:T(8,128)(2,1)} %e_ref.1, bf16[512,768]{1,0:T(8,128)(2,1)} %bitcast.3), custom_call_target="tpu_custom_call" | custom-call | tf_op jit(solution)/shard_map/pallas_call | solution.py:228
  96.2 2.7 %copy.4 = f32[1,512,768]{2,1,0:T(8,128)} copy(f32[1,512,768]{2,1,0:T(8,128)} %bitcast.2) | data formatting | bytes 3145728

commit v3 on v2

--- a/solution.py
+++ b/solution.py
@@ -8,7 +8,8 @@
 
 prior_weight = 1.0
 COLS = 2
-CHUNK = 512
+CHUNK = 1024
+LAG = 1
 MESH = pl.DeviceIdType.MESH
 
 
@@ -32,8 +33,13 @@
     return updated[None]
 
 
-def kernel(n_label, e_ref, c_ref, out_ref, table, expo, stats, sums, counts, norms,
-           load_sem, send_sem, recv_sem, sib_sem, stat_send, stat_recv):
+def combine(tops, totals):
+    top = jnp.max(tops, axis=0, keepdims=True)
+    return top, jnp.sum(totals * jnp.exp(tops - top), axis=0, keepdims=True)
+
+
+def kernel(n_label, e_ref, c_hbm, out_ref, c_ref, table, expo, stat_core, stat_y, stat_z, sums, counts, norms,
+           load_sem, c_sem, send_sem, recv_sem, sib_sem, stat_send, stat_recv):
     chunks, _, width = table.shape
     rows = e_ref.shape[0]
     half = width // 2
@@ -53,6 +59,8 @@
     ]
     for copy in loads:
         copy.start()
+    c_load = pltpu.make_async_copy(c_hbm, c_ref, c_sem)
+    c_load.start()
 
     barrier = pltpu.get_barrier_semaphore()
 
@@ -63,8 +71,6 @@
 
     lax.fori_loop(1, n_dev, greet, 0)
 
-    centroids = c_ref[...].astype(jnp.float32)
-    norms[...] = jnp.broadcast_to(0.5 * jnp.sum(centroids * centroids, axis=1, keepdims=True), norms.shape)
     sums[...] = jnp.zeros_like(sums)
     counts[...] = jnp.zeros_like(counts)
     pltpu.make_async_copy(table.at[:, pl.ds(0, rows), :], table.at[:, pl.ds(0, rows), :], load_sem).wait()
@@ -78,9 +84,11 @@
             src_ref=piece(j, index), dst_ref=piece(j, index), send_sem=send_sem.at[kind],
             recv_sem=recv_sem.at[j, index], device_id={"label": target}, device_id_type=MESH)
 
-    def sibling(j, index):
+    def sibling(j, index, size):
+        part = table.at[j, pl.ds(pl.multiple_of(index * rows, rows), size * rows),
+                        pl.ds(pl.multiple_of(core * half, half), half)]
         return pltpu.make_async_remote_copy(
-            src_ref=piece(j, index), dst_ref=piece(j, index), send_sem=send_sem.at[3],
+            src_ref=part, dst_ref=part, send_sem=send_sem.at[3],
             recv_sem=sib_sem.at[j], device_id={"cent": 1 - core}, device_id_type=MESH)
 
     def up(j, index):
@@ -109,7 +117,7 @@
             across(t, me)
 
         for d in range(1, n_z):
-            j = t - d
+            j = t - LAG * d
             for sign in (-1, 1):
                 far = z + sign * d
                 edge = jnp.logical_or(far == 0, far == n_z - 1)
@@ -124,10 +132,8 @@
                     def _():
                         across(j, index)
 
-                    sibling(j, index).start()
-
         for d in range(n_z):
-            j = t - d - 1
+            j = t - LAG * (d + 1)
             for sign in ((1,) if d == 0 else (-1, 1)):
                 far = z + sign * d
 
@@ -144,7 +150,10 @@
                     def _():
                         down(j, index)
 
-                    sibling(j, index).start()
+                    if d == 0:
+                        sibling(j, index, 1).start()
+                    else:
+                        sibling(j, far * COLS, COLS).start()
 
     def score(j):
         others = table.at[j, pl.ds(0, (n_label - 1) * rows), pl.ds(0, half)]
@@ -154,26 +163,36 @@
         top = jnp.max(scores, axis=0, keepdims=True)
         exponent = jnp.exp(scores - top)
         expo[j] = exponent
-        stats[j, self_id, 0:1, :] = top
-        stats[j, self_id, 1:2, :] = jnp.sum(exponent, axis=0, keepdims=True)
-
-        def tell(k, carry):
-            other = lax.rem(self_id + k, n_dev)
-            pltpu.make_async_remote_copy(
-                src_ref=stats.at[j, self_id], dst_ref=stats.at[j, self_id], send_sem=stat_send,
-                recv_sem=stat_recv.at[j], device_id={"label": other // 2, "cent": other % 2},
-                device_id_type=MESH).start()
-            return carry
-
-        lax.fori_loop(1, n_dev, tell, 0)
+        stat_core[j, core, 0:1, :] = top
+        stat_core[j, core, 1:2, :] = jnp.sum(exponent, axis=0, keepdims=True)
+        tell(stat_core, 0, j, core, {"cent": 1 - core})
+
+    def tell(buffer, stage, j, slot, target):
+        pltpu.make_async_remote_copy(
+            src_ref=buffer.at[j, slot], dst_ref=buffer.at[j, slot], send_sem=stat_send.at[stage],
+            recv_sem=stat_recv.at[stage, j], device_id=target, device_id_type=MESH).start()
+
+    def hear(buffer, stage, j, n):
+        others = buffer.at[j, pl.ds(0, n - 1)]
+        pltpu.make_async_copy(others, others, stat_recv.at[stage, j]).wait()
+        return combine(buffer[j, :, 0, :], buffer[j, :, 1, :])
+
+    def join_cores(j):
+        top, total = hear(stat_core, 0, j, 2)
+        stat_y[j, y, 0:1, :] = top
+        stat_y[j, y, 1:2, :] = total
+        tell(stat_y, 1, j, y, {"label": across_label})
+
+    def join_columns(j):
+        top, total = hear(stat_y, 1, j, COLS)
+        stat_z[j, z, 0:1, :] = top
+        stat_z[j, z, 1:2, :] = total
+        for k in range(1, n_z):
+            tell(stat_z, 2, j, z, {"label": lax.rem(z + k, n_z) * COLS + y})
 
     def absorb(j):
-        others = stats.at[j, pl.ds(0, n_dev - 1)]
-        pltpu.make_async_copy(others, others, stat_recv.at[j]).wait()
-        tops = stats[j, :, 0, :]
-        row_top = jnp.max(tops, axis=0, keepdims=True)
-        row_sum = jnp.sum(stats[j, :, 1, :] * jnp.exp(tops - row_top), axis=0, keepdims=True)
-        factor = jnp.exp(stats[j, self_id, 0:1, :] - row_top) / row_sum
+        row_top, row_sum = hear(stat_z, 2, j, n_z)
+        factor = jnp.exp(stat_core[j, core, 0:1, :] - row_top) / row_sum
         weights = (expo[j] * factor).astype(jnp.bfloat16)
         sums[...] += lax.dot_general(
             weights, table[j], (((1,), (1,)), ((), ())), preferred_element_type=jnp.float32)
@@ -182,23 +201,27 @@
             part += weights[:, k * 128:(k + 1) * 128].astype(jnp.float32)
         counts[...] = part
 
-    lag_a = n_z + 1
-    lag_b = n_z + 2
+    lag = LAG * n_z + 1
 
     def tick(t, carry):
         relay(t)
 
-        @pl.when(live(t - lag_a))
-        def _():
-            score(t - lag_a)
-
-        @pl.when(live(t - lag_b))
-        def _():
-            absorb(t - lag_b)
+        @pl.when(t == 0)
+        def _():
+            c_load.wait()
+            centroids = c_ref[...].astype(jnp.float32)
+            norms[...] = jnp.broadcast_to(0.5 * jnp.sum(centroids * centroids, axis=1, keepdims=True), norms.shape)
+
+        for later, step in enumerate((score, join_cores, join_columns, absorb)):
+            j = t - lag - later
+
+            @pl.when(live(j))
+            def _():
+                step(j)
 
         return carry
 
-    lax.fori_loop(0, chunks + lag_b, tick, 0)
+    lax.fori_loop(0, chunks + lag + 3, tick, 0)
 
     total = jnp.sum(counts[...], axis=1, keepdims=True)
     out_ref[...] = (sums[...] + prior_weight * c_ref[...].astype(jnp.float32)) / (total + prior_weight)
@@ -216,8 +239,9 @@
                 drain(1, 2 * (n_z - k) + 1)
             drain(2, 2 * n_z - (1 if k in (0, n_z - 1) else 2))
     drain(3, 2 * (n_label - 1))
-    told = stats.at[:, pl.ds(0, n_dev - 1)]
-    pltpu.make_async_copy(told, told, stat_send).wait()
+    for stage, (buffer, n) in enumerate(((stat_core, 2), (stat_y, COLS), (stat_z, n_z))):
+        told = buffer.at[:, pl.ds(0, n - 1)]
+        pltpu.make_async_copy(told, told, stat_send.at[stage]).wait()
 
 
 def fused_body(n_label, embeddings, centroids):
@@ -228,21 +252,25 @@
     updated = pl.pallas_call(
         functools.partial(kernel, n_label),
         out_shape=jax.ShapeDtypeStruct((count, depth), jnp.float32),
-        in_specs=[pl.BlockSpec(memory_space=pl.ANY), pl.BlockSpec(memory_space=pltpu.VMEM)],
+        in_specs=[pl.BlockSpec(memory_space=pl.ANY)] * 2,
         out_specs=pl.BlockSpec(memory_space=pltpu.VMEM),
         scratch_shapes=[
+            pltpu.VMEM((count, depth), jnp.bfloat16),
             pltpu.VMEM((chunks, depth, CHUNK), jnp.bfloat16),
             pltpu.VMEM((chunks, count, CHUNK), jnp.float32),
-            pltpu.VMEM((chunks, 2 * n_label, 2, CHUNK), jnp.float32),
+            pltpu.VMEM((chunks, 2, 2, CHUNK), jnp.float32),
+            pltpu.VMEM((chunks, COLS, 2, CHUNK), jnp.float32),
+            pltpu.VMEM((chunks, n_label // COLS, 2, CHUNK), jnp.float32),
             pltpu.VMEM((count, depth), jnp.float32),
             pltpu.VMEM((count, 128), jnp.float32),
             pltpu.VMEM((count, 128), jnp.float32),
             pltpu.SemaphoreType.DMA,
+            pltpu.SemaphoreType.DMA,
             pltpu.SemaphoreType.DMA((4,)),
             pltpu.SemaphoreType.DMA((chunks, n_label)),
             pltpu.SemaphoreType.DMA((chunks,)),
-            pltpu.SemaphoreType.DMA,
-            pltpu.SemaphoreType.DMA((chunks,)),
+            pltpu.SemaphoreType.DMA((3,)),
+            pltpu.SemaphoreType.DMA((3, chunks)),
         ],
         compiler_params=pltpu.CompilerParams(
             collective_id=0, has_side_effects=True, vmem_limit_bytes=60 * 1024 * 1024),

time: 99.1 us -> 90.2 us (0.910)
  Pallas kernels: 96.2 us -> 87.4 us
    pallas_call x1, Pallas kernels: 96.2 us -> 87.4 us  [fused_body(): pl.pallas_call(functools.partial(kernel, n_label), out_shape=jax.ShapeDty...]
where the time goes in v3:
time: 90.2 us; the launch traced here: 90.1 us
  Pallas kernels  87.4 us (97%)
  local copies, waits for them, and re-layouts  2.65 us (3%)
    pallas_call x1, Pallas kernels, fused_body(): pl.pallas_call(functools.partial(kernel, n_label), out_shape=jax.ShapeDty...  87.4 us
    unnamed x1, local copies, waits for them, and re-layouts  2.65 us

profile of v3, /device:TPU:0, one launch (start us, length us, event | category | flops | bytes accessed | tf_op | source)
XLA Modules:
  0.0 90.1 jit_solution(6636501931963982003)
XLA Ops:
  0.0 87.4 %shard_map.28 = f32[512,768]{1,0:T(8,128)} custom-call(bf16[96,8192]{1,0:T(8,128)(2,1)} %e_ref.1, bf16[512,768]{1,0:T(8,128)(2,1)} %bitcast.3), custom_call_target="tpu_custom_call" | custom-call | tf_op jit(solution)/shard_map/pallas_call | solution.py:252
  87.4 2.7 %copy.4 = f32[1,512,768]{2,1,0:T(8,128)} copy(f32[1,512,768]{2,1,0:T(8,128)} %bitcast.2) | data formatting | bytes 3145728
